TPU v7x, 512 devices: a whole 4x8x8 slice. The times are simulated.
512 devices in a mesh: dp: 4 (over z_lo), context: 128 (over x, z_hi, y, core).
Axes of the slice: x: 4, y: 8, z: 8 (z_hi: 2, z_lo: 4; z = z_hi * 4 + z_lo), core: 2. Of those that a mesh axis runs over, the one named last changes fastest.
Arguments:
- projected: bfloat16 [3, 16384, 8192], P(None, 'context', 'dp'), parts along dimension 2, may hold values from -6 to 6
- conv_weight: float32 [3, 3, 8192], P(None, None, 'dp'), parts along dimension 2, may hold values from -3 to 3
- bias: float32 [8192], P('dp'), parts along dimension 0, may hold values from -4 to 4
- spectrum: float32 [2, 256, 128, 512], P(None, 'context', None, 'dp'), parts along dimension 3, as said below
Outputs:
- block_out: float32 [16384, 8192], P('context', 'dp'), parts along dimension 1
There are 4 independent parts, one for each index of `dp`. A program takes and returns all parts, laid end to end along the dimension named above; each array names one. Nothing has to cross between parts.
Inputs may be any that keep to these rules, and one draw needn't show every extreme that they name: `spectrum`: each filter is real: for every k, entry k of the real part equals entry (32768 - k) mod 32768, and entry k of the imaginary part is the negative of that entry (frequency k stored at [., k mod 256, k // 256, .]).
All inputs are finite; a program needn't handle non-finite values.
Results may differ from a plain program's by a relative error of at most 0.0045.
Values may be sent and summed in bfloat16 or wider, within the bound.
A program may use at most 64 MiB of HBM per device.

v0:
```python
import math

import jax
import jax.numpy as jnp
import numpy as np
from jax import lax
from jax.sharding import PartitionSpec as P

COLS = 128
SHARE = 16
HIGHEST = lax.Precision.HIGHEST


def tables(data_rows):
    grid_rows = 2 * data_rows
    fft_len = grid_rows * COLS
    c = np.arange(grid_rows)
    a = np.arange(data_rows)
    b = np.arange(COLS)
    rows = 2.0 * np.pi * (np.outer(c, a) % grid_rows) / grid_rows
    cols = 2.0 * np.pi * (np.outer(b, b) % COLS) / COLS
    twist = 2.0 * np.pi * (np.outer(c, b) % fft_len) / fft_len
    rc, rs = np.cos(rows), np.sin(rows)
    cc, cs = np.cos(cols), np.sin(cols)
    first = np.block([[rc, rs], [-rs, rc]])
    mid = np.block([[cc, -cs], [cs, cc]])
    back = np.block([[cc, cs], [-cs, cc]])
    last = np.block([[rc.T, -rs.T], [rs.T, rc.T]]) / fft_len
    made = (first, mid, back, last, np.cos(twist), np.sin(twist))
    return tuple(t.astype(np.float32) for t in made)


def from_behind(shard, axis, by):
    devices = lax.axis_size(axis)
    pairs = [(i, i + by) for i in range(devices) if 0 <= i + by < devices]
    return lax.ppermute(shard, axis, pairs)


def local(projected, conv_weight, bias, spectrum):
    group = lax.axis_size("context")
    local_len = projected.shape[1]
    channels = projected.shape[2]
    half = SHARE // 2
    grid_rows = 2 * group
    left_rim = from_behind(projected[:, local_len - 2 :, :], "context", 1)
    extended = jnp.concatenate([left_rim, projected], axis=1).astype(jnp.float32)
    shorts = (
        conv_weight[:, 0:1, :] * extended[:, 2:, :]
        + conv_weight[:, 1:2, :] * extended[:, 1:-1, :]
        + conv_weight[:, 2:3, :] * extended[:, :-2, :]
    )
    gated = (shorts[1] * shorts[2]).astype(jnp.bfloat16)
    signal = jnp.transpose(gated).reshape(group, SHARE, COLS)
    filters = jnp.transpose(spectrum.astype(jnp.bfloat16), (3, 0, 1, 2)).reshape(group, 4, COLS)
    sent = jnp.concatenate([signal, filters], axis=1)
    held = lax.all_to_all(sent, "context", split_axis=0, concat_axis=0, tiled=True)
    first, mid, back, last, twist_cos, twist_sin = tables(group)
    x = held[:, :SHARE, :].astype(jnp.float32)
    f = held[:, SHARE:, :].astype(jnp.float32).reshape(group, 2, 2, COLS)
    fr = f[:, 0].reshape(grid_rows, 1, COLS)
    fi = f[:, 1].reshape(grid_rows, 1, COLS)
    x = jnp.concatenate([x[:, :half], x[:, half:]], axis=0)
    tc, ts = twist_cos[:, None, :], twist_sin[:, None, :]
    y = jnp.einsum("ca,ahb->chb", first, x, precision=HIGHEST)
    yr, yi = y[:grid_rows], y[grid_rows:]
    z = jnp.concatenate([yr * tc + yi * ts, yi * tc - yr * ts], axis=2)
    g = jnp.einsum("chb,bd->chd", z, mid, precision=HIGHEST)
    gr, gi = g[:, :, :COLS], g[:, :, COLS:]
    p = jnp.concatenate([gr * fr - gi * fi, gr * fi + gi * fr], axis=2)
    q = jnp.einsum("chd,db->chb", p, back, precision=HIGHEST)
    qr, qi = q[:, :, :COLS], q[:, :, COLS:]
    r = jnp.concatenate([qr * tc - qi * ts, qi * tc + qr * ts], axis=0)
    out = jnp.einsum("ac,chb->ahb", last, r, precision=HIGHEST)
    out = jnp.concatenate([out[:group], out[group:]], axis=1).astype(jnp.bfloat16)
    conv = lax.all_to_all(out, "context", split_axis=0, concat_axis=0, tiled=True)
    long_conv = jnp.transpose(conv.reshape(channels, local_len)).astype(jnp.float32)
    return shorts[0] * (long_conv + bias[None, :] * gated.astype(jnp.float32))


def solution(mesh):
    placed = (
        P(None, "context", "dp"),
        P(None, None, "dp"),
        P("dp"),
        P(None, "context", None, "dp"),
    )
    return jax.shard_map(
        local, mesh=mesh, in_specs=placed, out_specs=P("context", "dp"), check_vma=False
    )
```

profile of v0, /device:TPU:1, one launch (start us, length us, event | category | flops | bytes accessed | tf_op | source)
XLA Modules:
  0.0 117.5 jit_solution(17504333801412029954)
XLA Ops:
  0.0 0.9 slice.75
  0.9 4.6 %collective-permute-start = (bf16[3,2,2048]{2,1,0:T(2,128)(2,1)S(1)}, bf16[3,2,2048]{2,1,0:T(2,128)(2,1)S(1)}, u32[]{:S(2)}, u32[]{:S(2)}) collective-permute-start(bf16[3,2,2048]{2,1,0:T(2,128)(2,1)S(1)} %slice.75), channel_id=1, source_target_pairs={{0,1},{1,2},{2,3},{3,4},{4,5},{5,6},{6,7},{7,8},{8,9},{9,10},{10,1... | collective-permute-start | bytes 73736 | tf_op jit(solution)/shard_map/ppermute | solution.py:36
  5.5 1.1 fusion.26
  6.7 1.0 convert_bitcast_fusion.1
  7.6 1.9 %copy.31 = bf16[3,128,2048]{1,2,0:T(8,128)(2,1)S(1)} copy(bf16[3,128,2048]{2,1,0:T(8,128)(2,1)} %param.10) | data formatting | bytes 3145728 | tf_op args[0]
  9.7 0.9 copy.30
  10.6 1.1 maximum_convert_fusion
  11.8 4.7 %fusion = f32[3,128,2048]{1,2,0:T(8,128)S(1)} fusion(f32[3,130,2048]{1,2,0:T(8,128)S(1)} %maximum_convert_fusion, f32[3,2048]{1,0:T(4,128)S(1)} %get-tuple-element.20, f32[3,2048]{1,0:T(4,128)S(1)} %get-tuple-element.21, f32[3,2048]{1,0:T(4,128)S(1)} %bitcast.54), kind=kLoop, calls=%fused_computation.1 | loop fusion | flops 3932160 | bytes 12656640 | tf_op jit(solution)/shard_map/add | solution.py:48
  16.7 47.6 %all_to_all.10 = bf16[128,20,128]{2,1,0:T(8,128)(2,1)S(1)} all-to-all(bf16[128,20,128]{2,1,0:T(8,128)(2,1)S(1)} %pad_maximum_fusion.1), channel_id=1, replica_groups=mesh['dp'=4,'context'=128] {'context'}, dimensions={0} | all-to-all | bytes 1310720 | tf_op jit(solution)/shard_map/all_to_all | solution.py:56
  64.3 0.9 copy-done
  65.2 0.8 slice.104
  66.0 2.2 %copy.52 = bf16[128,16,128]{0,2,1:T(8,128)(2,1)} copy(bf16[128,16,128]{2,1,0:T(8,128)(2,1)} %slice.104) | data formatting | bytes 1048576
  68.3 2.1 %fusion.24 = (f32[128,8,128]{0,2,1:T(8,128)}, f32[128,8,128]{0,2,1:T(8,128)}) fusion(bf16[128,16,128]{0,2,1:T(8,128)(2,1)} %copy.52), kind=kLoop, calls=%fused_computation.42 | loop fusion | bytes 2097152 | tf_op jit(solution)/shard_map/slice | solution.py:62
  70.4 1.0 slice.110
  71.7 1.3 %pad_maximum_fusion = f32[256,8,128]{0,2,1:T(8,128)S(1)} fusion(f32[128,8,128]{0,2,1:T(8,128)} %get-tuple-element.14, f32[128,8,128]{0,2,1:T(8,128)} %get-tuple-element.13), kind=kLoop, calls=%fused_computation.23 | loop fusion | flops 262144 | bytes 2097152 | tf_op jit(solution)/shard_map/concatenate | solution.py:62
  73.1 1.9 %fusion.27 = f32[512,1024]{0,1:S(1)} fusion(f32[512,256]{1,0:T(8,128)S(1)} %copy-done.1, f32[256,1024]{0,1:T(8,128)S(1)} %bitcast.48), kind=kOutput, calls=%fused_computation.45 | convolution fusion | flops 1610612736 | bytes 3670016
  75.9 2.0 %fusion.2 = f32[256,8,256]{0,2,1:T(8,128)S(1)} fusion(f32[256,256,1]{0,1,2:T(8,128)S(1)} %copy-done.6, f32[256,8,128]{0,2,1:T(8,128)S(1)} %get-tuple-element.10, f32[256,8,128]{0,2,1:T(8,128)S(1)} %get-tuple-element.9), kind=kOutput, calls=%fused_computation.6 | convolution fusion | flops 1611137024 | bytes 4456448 | tf_op jit(solution)/shard_map/chb,bd->chd/dot_general | solution.py:67
  78.3 0.7 copy-done.5
  78.9 2.1 %fusion.6 = f32[256,8,256]{0,2,1:T(8,128)S(1)} fusion(f32[256,256,1]{1,0,2:T(8,128)S(1)} %copy-done.5, f32[256,8,128]{0,2,1:T(8,128)S(1)} %get-tuple-element.8, f32[256,8,128]{0,2,1:T(8,128)S(1)} %get-tuple-element.7), kind=kOutput, calls=%fused_computation.10 | convolution fusion | flops 1611137024 | bytes 4456448 | tf_op jit(solution)/shard_map/chd,db->chb/dot_general | solution.py:70
  81.3 0.8 copy-done.4
  82.1 1.9 %fusion.14 = bf16[256,8,128]{2,0,1:T(8,128)(2,1)S(1)} fusion(f32[256,512,1]{1,0,2:T(8,128)S(1)} %copy-done.4, f32[256,8,128]{0,2,1:T(8,128)S(1)} %get-tuple-element.6, f32[256,8,128]{0,2,1:T(8,128)S(1)} %get-tuple-element.5), kind=kOutput, calls=%fused_computation.18 | convolution fusion | flops 1611399168 | bytes 3145728 | tf_op jit(solution)/shard_map/ac,chb->ahb/dot_general | solution.py:73
  84.5 29.1 %all_to_all.11 = bf16[128,16,128]{2,1,0:T(8,128)(2,1)S(1)} all-to-all(bf16[128,16,128]{2,1,0:T(8,128)(2,1)S(1)} %copy.43), channel_id=1, replica_groups=mesh['dp'=4,'context'=128] {'context'}, dimensions={0} | all-to-all | bytes 1048576 | tf_op jit(solution)/shard_map/all_to_all | solution.py:75
  113.6 1.4 %fusion.18 = f32[128,2048]{0,1:T(8,128)} fusion(f32[3,128,2048]{1,2,0:T(8,128)S(1)} %fusion, bf16[128,16,128]{2,1,0:T(8,128)(2,1)S(1)} %all_to_all.11, f32[2048]{0:T(1024)S(1)} %copy-done.7), kind=kLoop, calls=%fused_computation.22 | loop fusion | flops 1835008 | bytes 4726784 | tf_op jit(solution)/shard_map/mul | solution.py:77
  114.9 2.5 %copy.44 = f32[128,2048]{1,0:T(8,128)} copy(f32[128,2048]{0,1:T(8,128)} %fusion.18) | data formatting | bytes 2097152 | tf_op jit(solution)/shard_map/mul | solution.py:77
  (28 shorter events, 2.7 us)
Async XLA Ops:
  0.9 8.8 %collective-permute-start = (bf16[3,2,2048]{2,1,0:T(2,128)(2,1)S(1)}, bf16[3,2,2048]{2,1,0:T(2,128)(2,1)S(1)}, u32[]{:S(2)}, u32[]{:S(2)}) collective-permute-start(bf16[3,2,2048]{2,1,0:T(2,128)(2,1)S(1)} %slice.75), channel_id=1, source_target_pairs={{0,1},{1,2},{2,3},{3,4},{4,5},{5,6},{6,7},{7,8},{8,9},{9,10},{10,1... | collective-permute-start | bytes 73736 | tf_op jit(solution)/shard_map/ppermute | solution.py:36
  64.3 0.9 copy-start
  71.7 1.4 %copy-start.1 = (f32[512,256]{1,0:T(8,128)S(1)}, f32[512,256]{1,0:T(8,128)}, u32[]{:S(2)}) copy-start(f32[512,256]{1,0:T(8,128)} %constant.12.clone) | copy-start | bytes 1572868
  73.1 1.9 %copy-start.2 = (f32[256,128]{0,1:T(8,128)S(1)}, f32[256,128]{0,1:T(8,128)}, u32[]{:S(2)}) copy-start(f32[256,128]{0,1:T(8,128)} %constant.19) | copy-start | bytes 393220
  73.1 1.9 %copy-start.3 = (f32[256,128]{0,1:T(8,128)S(1)}, f32[256,128]{0,1:T(8,128)}, u32[]{:S(2)}) copy-start(f32[256,128]{0,1:T(8,128)} %constant.20) | copy-start | bytes 393220
  75.0 1.0 copy-start.6
  78.0 1.0 copy-start.5
  81.0 1.0 copy-start.4
  84.0 29.6 %copy-start.7 = (f32[2048]{0:T(1024)S(1)}, f32[2048]{0:T(1024)}, u32[]{:S(2)}) copy-start(f32[2048]{0:T(1024)} %param.12) | copy-start | bytes 24580
where the time goes:
time: 118 us; the launch traced here: 117 us
  blocking collectives  76.7 us (65%)
  local copies, waits for them, and re-layouts  17.4 us (15%)
  other arithmetic  10.6 us (9%)
  matrix products  7.89 us (7%)
  starting transfers between devices  4.58 us (4%)
    all_to_all x1, blocking collectives, local(): lax.all_to_all(sent, 'context', split_axis=0, concat_axis=0, tiled=True)  47.6 us
    all_to_all x1, blocking collectives, local(): lax.all_to_all(out, 'context', split_axis=0, concat_axis=0, tiled=True)  29.1 us
    unnamed x20, local copies, waits for them, and re-layouts  7.17 us
    add x1, other arithmetic, local(): conv_weight[:, 0:1, :] * extended[:, 2:, :]  4.67 us
    ppermute x1, starting transfers between devices, from_behind(): return lax.ppermute(shard, axis, pairs)  4.58 us
    mul x1, local copies, waits for them, and re-layouts, local(): return shorts[0] * (long_conv + bias[None, :] * gated.astype(jnp.float32))  2.53 us
  transfers between devices with their start and end apart: 1, of which 0 were waited for; matrix products, arithmetic and copies ran while one was open for 4% of the time, Pallas kernels for 0%

commit v1 on v0

v1 whole, which is shorter than its diff:
```python
import functools

import jax
import jax.numpy as jnp
import numpy as np
from jax import lax
from jax.experimental import pallas as pl
from jax.experimental.pallas import tpu as pltpu
from jax.sharding import PartitionSpec as P

COLS = 128
SHARE = 16
HALF = SHARE // 2


def tables(data_rows):
    grid_rows = 2 * data_rows
    fft_len = grid_rows * COLS
    c = np.concatenate([np.arange(0, grid_rows, 2), np.arange(1, grid_rows, 2)])
    a = np.arange(data_rows)
    b = np.arange(COLS)
    rows = 2.0 * np.pi * (np.outer(c, a) % grid_rows) / grid_rows
    cols = 2.0 * np.pi * (np.outer(b, b) % COLS) / COLS
    twist = 2.0 * np.pi * (np.outer(c, b) % fft_len) / fft_len
    rc, rs = np.cos(rows), np.sin(rows)
    cc, cs = np.cos(cols), np.sin(cols)
    first = np.block([[rc, rs], [-rs, rc]])
    mid = np.block([[cc, -cs], [cs, cc]])
    back = np.block([[cc, cs], [-cs, cc]])
    last = np.block([[rc.T, -rs.T], [rs.T, rc.T]]) / fft_len
    split = []
    for table in (first, mid, back, last):
        table = table.astype(np.float32)
        high = table.astype(jnp.bfloat16)
        split += [high, (table - high.astype(np.float32)).astype(jnp.bfloat16)]
    return split + [np.cos(twist).astype(np.float32), np.sin(twist).astype(np.float32)]


def mm(x, y):
    return jnp.dot(x, y, preferred_element_type=jnp.float32)


def halves(x):
    high = x.astype(jnp.bfloat16)
    return high, (x - high.astype(jnp.float32)).astype(jnp.bfloat16)


def transform(xs, sp, ys, tabs):
    fh, fl, mh, ml, bh, bl, lh, ll, tc_ref, ts_ref = tabs
    tc, ts = tc_ref[...], ts_ref[...]
    grid_rows = tc.shape[0]
    fr = jnp.concatenate([sp[:, 0, :], sp[:, 1, :]], axis=0)
    fi = jnp.concatenate([sp[:, 2, :], sp[:, 3, :]], axis=0)
    for h in range(0, HALF, 2):
        pair = [
            jnp.concatenate([xs[:, i, :], xs[:, i + HALF, :]], axis=0).astype(jnp.bfloat16)
            for i in (h, h + 1)
        ]
        x = jnp.concatenate(pair, axis=1)
        y = mm(fh[...], x) + mm(fl[...], x)
        turned = []
        for i in range(2):
            yr = y[:grid_rows, i * COLS : (i + 1) * COLS]
            yi = y[grid_rows:, i * COLS : (i + 1) * COLS]
            zh, zl = halves(jnp.concatenate([yr * tc + yi * ts, yi * tc - yr * ts], axis=1))
            g = mm(zh, mh[...]) + mm(zl, mh[...]) + mm(zh, ml[...])
            gr, gi = g[:, :COLS], g[:, COLS:]
            ph, plo = halves(jnp.concatenate([gr * fr - gi * fi, gr * fi + gi * fr], axis=1))
            q = mm(ph, bh[...]) + mm(plo, bh[...]) + mm(ph, bl[...])
            qr, qi = q[:, :COLS], q[:, COLS:]
            turned.append(jnp.concatenate([qr * tc - qi * ts, qi * tc + qr * ts], axis=0))
        rh, rl = halves(jnp.concatenate(turned, axis=1))
        o = mm(lh[...], rh) + mm(lh[...], rl) + mm(ll[...], rh)
        n = grid_rows // 2
        for i in range(2):
            ys[:, h + i, :] = o[:n, i * COLS : (i + 1) * COLS]
            ys[:, h + i + HALF, :] = o[n:, i * COLS : (i + 1) * COLS]


def kernel(group, proj, weight, bias, spec, *refs):
    tabs = refs[:10]
    out = refs[10]
    (tail, halo, q_keep, gated, xs, ys, sf, sig_out, sig_in, spec_out, spec_in, conv_out, conv_in,
     send_sems, recv_sems, own_sems) = refs[11:]
    me = lax.axis_index("context")
    rows = proj.shape[1]
    blocks = proj.shape[2] // COLS
    per = COLS // SHARE

    def copy_to(src, dst, number, peer):
        return pltpu.make_async_remote_copy(
            src_ref=src,
            dst_ref=dst,
            send_sem=send_sems.at[number],
            recv_sem=recv_sems.at[number],
            device_id={"context": peer},
            device_id_type=pl.DeviceIdType.MESH,
        )

    def await_all(src, dst, number):
        some = pl.ds(0, group - 1)
        pltpu.make_async_copy(src.at[some], dst.at[some], send_sems.at[number]).wait()
        pltpu.make_async_copy(src.at[some], dst.at[some], recv_sems.at[number]).wait()

    halo[...] = jnp.zeros_like(halo)
    barrier = pltpu.get_barrier_semaphore()

    @pl.loop(1, group)
    def _(k):
        pl.semaphore_signal(
            barrier,
            inc=1,
            device_id={"context": lax.rem(me + k, group)},
            device_id_type=pl.DeviceIdType.MESH,
        )

    ends = [proj[j, rows - 16 :, :].astype(jnp.float32)[14:16, :] for j in range(3)]
    ends.append(jnp.zeros_like(ends[0]))
    tail[...] = jnp.concatenate(ends, axis=0).astype(jnp.bfloat16)
    for i in range(2):
        for j in range(2):
            sf[:, 2 * i + j, :] = jnp.transpose(spec[i, j])
    spec_out[...] = sf[...].astype(jnp.bfloat16)
    pl.semaphore_wait(barrier, group - 1)

    @pl.when(me < group - 1)
    def _():
        copy_to(tail, halo, 0, me + 1).start()

    own_spec = pltpu.make_async_copy(spec_out.at[me], spec_in.at[me], own_sems.at[0])
    own_spec.start()

    @pl.loop(1, group)
    def _(k):
        peer = lax.rem(me + k, group)
        copy_to(spec_out.at[peer], spec_in.at[me], 1, peer).start()

    @pl.when(me > 0)
    def _():
        copy_to(tail, halo, 0, me).wait_recv()

    @pl.when(me < group - 1)
    def _():
        copy_to(tail, halo, 0, me).wait_send()

    row = lax.broadcasted_iota(jnp.int32, (rows, COLS), 0)

    @pl.loop(0, blocks)
    def _(step):
        block = lax.rem(step + me // per, blocks)
        lanes = pl.ds(pl.multiple_of(block * COLS, COLS), COLS)
        edge = halo[:, lanes].astype(jnp.float32)
        shorts = []
        for j in range(3):
            x = proj[j, :, lanes].astype(jnp.float32)
            e2, e1 = edge[2 * j : 2 * j + 1, :], edge[2 * j + 1 : 2 * j + 2, :]
            x1 = jnp.where(row == 0, e1, pltpu.roll(x, 1, 0))
            x2 = jnp.where(row == 0, e2, jnp.where(row == 1, e1, pltpu.roll(x, 2, 0)))
            w = weight[j, :, lanes]
            shorts.append(w[0:1] * x + w[1:2] * x1 + w[2:3] * x2)
        q_keep[:, lanes] = shorts[0]
        g = (shorts[1] * shorts[2]).astype(jnp.bfloat16)
        gated[:, lanes] = g
        turned = jnp.transpose(g.astype(jnp.float32)).astype(jnp.bfloat16)
        sig_out[pl.ds(block * per, per)] = turned.reshape(per, SHARE, COLS)

    own_sig = pltpu.make_async_copy(sig_out.at[me], sig_in.at[me], own_sems.at[1])
    own_sig.start()

    @pl.loop(1, group)
    def _(k):
        peer = lax.rem(me + k, group)
        copy_to(sig_out.at[peer], sig_in.at[me], 2, peer).start()

    await_all(spec_out, spec_in, 1)
    own_spec.wait()
    sf[...] = spec_in[...].astype(jnp.float32)
    await_all(sig_out, sig_in, 2)
    own_sig.wait()
    xs[...] = sig_in[...].astype(jnp.float32)
    transform(xs, sf, ys, tabs)
    conv_out[...] = ys[...].astype(jnp.bfloat16)

    own_conv = pltpu.make_async_copy(conv_out.at[me], conv_in.at[me], own_sems.at[2])
    own_conv.start()

    @pl.loop(1, group)
    def _(k):
        peer = lax.rem(me + k, group)
        copy_to(conv_out.at[peer], conv_in.at[me], 3, peer).start()

    await_all(conv_out, conv_in, 3)
    own_conv.wait()

    @pl.loop(0, blocks)
    def _(block):
        lanes = pl.ds(pl.multiple_of(block * COLS, COLS), COLS)
        conv = conv_in[pl.ds(block * per, per)].reshape(COLS, COLS).astype(jnp.float32)
        skip = bias[:, lanes] * gated[:, lanes].astype(jnp.float32)
        out[:, lanes] = q_keep[:, lanes] * (jnp.transpose(conv) + skip)


def local(projected, conv_weight, bias, spectrum):
    group = lax.axis_size("context")
    rows, channels = projected.shape[1:]
    bf16, f32 = jnp.bfloat16, jnp.float32
    made = tables(group)
    vmem = pl.BlockSpec(memory_space=pltpu.VMEM)
    return pl.pallas_call(
        functools.partial(kernel, group),
        out_shape=jax.ShapeDtypeStruct((rows, channels), f32),
        in_specs=[vmem] * (4 + len(made)),
        out_specs=vmem,
        scratch_shapes=[
            pltpu.VMEM((8, channels), bf16),
            pltpu.VMEM((8, channels), bf16),
            pltpu.VMEM((rows, channels), f32),
            pltpu.VMEM((rows, channels), bf16),
            pltpu.VMEM((group, SHARE, COLS), f32),
            pltpu.VMEM((group, SHARE, COLS), f32),
            pltpu.VMEM((group, 4, COLS), f32),
            pltpu.VMEM((group, SHARE, COLS), bf16),
            pltpu.VMEM((group, SHARE, COLS), bf16),
            pltpu.VMEM((group, 4, COLS), bf16),
            pltpu.VMEM((group, 4, COLS), bf16),
            pltpu.VMEM((group, SHARE, COLS), bf16),
            pltpu.VMEM((group, SHARE, COLS), bf16),
            pltpu.SemaphoreType.DMA((4,)),
            pltpu.SemaphoreType.DMA((4,)),
            pltpu.SemaphoreType.DMA((3,)),
        ],
        compiler_params=pltpu.CompilerParams(collective_id=0, has_side_effects=True),
        name="hyena",
    )(projected, conv_weight, bias[None, :], spectrum, *made)


def solution(mesh):
    placed = (
        P(None, "context", "dp"),
        P(None, None, "dp"),
        P("dp"),
        P(None, "context", None, "dp"),
    )
    return jax.shard_map(
        local, mesh=mesh, in_specs=placed, out_specs=P("context", "dp"), check_vma=False
    )
```

time: 118 us -> 69.2 us (0.59)
  blocking collectives: 76.7 us -> 0 us
  Pallas kernels: 0 us -> 66.7 us
  local copies, waits for them, and re-layouts: 17.4 us -> 2.3 us
  other arithmetic: 10.6 us -> 0 us
  matrix products: 7.89 us -> 0 us
  starting transfers between devices: 4.58 us -> 0 us
    all_to_all x2 -> x0, blocking collectives: 76.7 us -> none  [the longest x1 47.6 us: local(): lax.all_to_all(sent, 'context', split_axis=0, concat_axis=0, tiled=True)]
    pallas_call x0 -> x1, Pallas kernels: none -> 66.7 us  [local(): pl.pallas_call(functools.partial(kernel, group), out_shape=jax.ShapeDtype...]
    slice x7 -> x0, local copies, waits for them, and re-layouts: 6.13 us -> none  [the longest x1 2.14 us: local(): x = jnp.concatenate([x[:, :half], x[:, half:]], axis=0)]
    dot_general x3 -> x0, matrix products: 6.01 us -> none  [the longest x1 2.06 us: local(): q = jnp.einsum('chd,db->chb', p, back, precision=HIGHEST)]
    add x2 -> x0, other arithmetic: 4.95 us -> none  [the longest x1 4.67 us: local(): conv_weight[:, 0:1, :] * extended[:, 2:, :]]
    unnamed x20 -> x1, local copies, waits for them, and re-layouts: 7.17 us -> 2.3 us
    ppermute x1 -> x0, starting transfers between devices: 4.58 us -> none  [from_behind(): return lax.ppermute(shard, axis, pairs)]
    mul x3 -> x0, local copies, waits for them, and re-layouts: 2.72 us -> none  [the longest x1 2.53 us: local(): return shorts[0] * (long_conv + bias[None, :] * gated.astype(jnp.float32))]
  transfers between devices with their start and end apart: 1 -> 0, of which waited for: 0 -> 0; matrix products, arithmetic and copies ran while one was open for 4% -> 0% of each run, Pallas kernels for 0% -> 0%
where the time goes in v1:
time: 69.2 us; the launch traced here: 69 us
  Pallas kernels  66.7 us (96%)
  local copies, waits for them, and re-layouts  2.3 us (3%)
    pallas_call x1, Pallas kernels, local(): pl.pallas_call(functools.partial(kernel, group), out_shape=jax.ShapeDtype...  66.7 us
    unnamed x1, local copies, waits for them, and re-layouts  2.3 us

profile of v1, /device:TPU:1, one launch (start us, length us, event | category | flops | bytes accessed | tf_op | source)
XLA Modules:
  0.0 69.0 jit_solution(3134052861194101505)
XLA Ops:
  0.0 66.7 %hyena.1 = f32[128,2048]{1,0:T(8,128)} custom-call(bf16[3,128,2048]{2,1,0:T(8,128)(2,1)} %proj.1, f32[3,3,2048]{2,1,0:T(4,128)} %weight.1, f32[1,2048]{1,0:T(1,128)} %bitcast.1, f32[2,2,128,128]{3,2,1,0:T(8,128)} %spec.1, bf16[512,256]{1,0:T(8,128)(2,1)} %constant.20.clone.refs_0_, bf16[512,256]{1,0:T(8,128)(2,1)} %constant.21.clone.refs_1_, ...), custom_call_target="tpu_custom_call" | custom-call | tf_op jit(solution)/shard_map/hyena/pallas_call | solution.py:209
  66.7 2.3 %copy.16 = f32[128,2048]{1,0:T(8,128)} copy(f32[128,2048]{1,0:T(8,128)} %hyena.1) | data formatting | bytes 2097152

commit v2 on v1

--- a/solution.py
+++ b/solution.py
@@ -10,7 +10,9 @@
 
 COLS = 128
 SHARE = 16
-HALF = SHARE // 2
+PARTS = 2
+PIECE = SHARE // PARTS
+HALF = PIECE // 2
 
 
 def tables(data_rows):
@@ -40,11 +42,6 @@
     return jnp.dot(x, y, preferred_element_type=jnp.float32)
 
 
-def halves(x):
-    high = x.astype(jnp.bfloat16)
-    return high, (x - high.astype(jnp.float32)).astype(jnp.bfloat16)
-
-
 def transform(xs, sp, ys, tabs):
     fh, fl, mh, ml, bh, bl, lh, ll, tc_ref, ts_ref = tabs
     tc, ts = tc_ref[...], ts_ref[...]
@@ -62,15 +59,17 @@
         for i in range(2):
             yr = y[:grid_rows, i * COLS : (i + 1) * COLS]
             yi = y[grid_rows:, i * COLS : (i + 1) * COLS]
-            zh, zl = halves(jnp.concatenate([yr * tc + yi * ts, yi * tc - yr * ts], axis=1))
-            g = mm(zh, mh[...]) + mm(zl, mh[...]) + mm(zh, ml[...])
+            z = jnp.concatenate([yr * tc + yi * ts, yi * tc - yr * ts], axis=1)
+            z = z.astype(jnp.bfloat16)
+            g = mm(z, mh[...]) + mm(z, ml[...])
             gr, gi = g[:, :COLS], g[:, COLS:]
-            ph, plo = halves(jnp.concatenate([gr * fr - gi * fi, gr * fi + gi * fr], axis=1))
-            q = mm(ph, bh[...]) + mm(plo, bh[...]) + mm(ph, bl[...])
+            p = jnp.concatenate([gr * fr - gi * fi, gr * fi + gi * fr], axis=1)
+            p = p.astype(jnp.bfloat16)
+            q = mm(p, bh[...]) + mm(p, bl[...])
             qr, qi = q[:, :COLS], q[:, COLS:]
             turned.append(jnp.concatenate([qr * tc - qi * ts, qi * tc + qr * ts], axis=0))
-        rh, rl = halves(jnp.concatenate(turned, axis=1))
-        o = mm(lh[...], rh) + mm(lh[...], rl) + mm(ll[...], rh)
+        r = jnp.concatenate(turned, axis=1).astype(jnp.bfloat16)
+        o = mm(lh[...], r) + mm(ll[...], r)
         n = grid_rows // 2
         for i in range(2):
             ys[:, h + i, :] = o[:n, i * COLS : (i + 1) * COLS]
@@ -79,9 +78,9 @@
 
 def kernel(group, proj, weight, bias, spec, *refs):
     tabs = refs[:10]
-    out = refs[10]
-    (tail, halo, q_keep, gated, xs, ys, sf, sig_out, sig_in, spec_out, spec_in, conv_out, conv_in,
-     send_sems, recv_sems, own_sems) = refs[11:]
+    q_keep, total = refs[10:12]
+    (tail, halo, gated, xs, ys, sf, sig_out, sig_in, spec_out, spec_in, conv_out, conv_in,
+     send_sems, recv_sems, own_sems) = refs[12:]
     me = lax.axis_index("context")
     rows = proj.shape[1]
     blocks = proj.shape[2] // COLS
@@ -97,10 +96,18 @@
             device_id_type=pl.DeviceIdType.MESH,
         )
 
-    def await_all(src, dst, number):
+    def all_copies(src, dst, sem):
         some = pl.ds(0, group - 1)
-        pltpu.make_async_copy(src.at[some], dst.at[some], send_sems.at[number]).wait()
-        pltpu.make_async_copy(src.at[some], dst.at[some], recv_sems.at[number]).wait()
+        return pltpu.make_async_copy(src.at[some], dst.at[some], sem)
+
+    def keep(src, dst, number):
+        return pltpu.make_async_copy(src.at[me], dst.at[me], own_sems.at[number])
+
+    def to_all(src, dst, number):
+        @pl.loop(1, group)
+        def _(k):
+            peer = lax.rem(me + k, group)
+            copy_to(src.at[peer], dst.at[me], number, peer).start()
 
     halo[...] = jnp.zeros_like(halo)
     barrier = pltpu.get_barrier_semaphore()
@@ -127,13 +134,10 @@
     def _():
         copy_to(tail, halo, 0, me + 1).start()
 
-    own_spec = pltpu.make_async_copy(spec_out.at[me], spec_in.at[me], own_sems.at[0])
+    own_spec = keep(spec_out, spec_in, 0)
     own_spec.start()
 
-    @pl.loop(1, group)
-    def _(k):
-        peer = lax.rem(me + k, group)
-        copy_to(spec_out.at[peer], spec_in.at[me], 1, peer).start()
+    to_all(spec_out, spec_in, 1)
 
     @pl.when(me > 0)
     def _():
@@ -142,6 +146,14 @@
     @pl.when(me < group - 1)
     def _():
         copy_to(tail, halo, 0, me).wait_send()
+
+    def send_block(block):
+        for i in range(per):
+            peer = block * per + lax.rem(me + i, per)
+
+            @pl.when(peer != me)
+            def _():
+                copy_to(sig_out.at[0, peer], sig_in.at[0, me], 2, peer).start()
 
     row = lax.broadcasted_iota(jnp.int32, (rows, COLS), 0)
 
@@ -161,43 +173,52 @@
         q_keep[:, lanes] = shorts[0]
         g = (shorts[1] * shorts[2]).astype(jnp.bfloat16)
         gated[:, lanes] = g
-        turned = jnp.transpose(g.astype(jnp.float32)).astype(jnp.bfloat16)
-        sig_out[pl.ds(block * per, per)] = turned.reshape(per, SHARE, COLS)
-
-    own_sig = pltpu.make_async_copy(sig_out.at[me], sig_in.at[me], own_sems.at[1])
-    own_sig.start()
-
-    @pl.loop(1, group)
-    def _(k):
-        peer = lax.rem(me + k, group)
-        copy_to(sig_out.at[peer], sig_in.at[me], 2, peer).start()
-
-    await_all(spec_out, spec_in, 1)
+        turned = jnp.transpose(g.astype(jnp.float32))
+        turned = turned.reshape(per, PARTS, PIECE, COLS)
+        for part in range(PARTS):
+            sig_out[part, pl.ds(block * per, per)] = turned[:, part].astype(jnp.bfloat16)
+
+        @pl.when(step > 0)
+        def _():
+            send_block(lax.rem(step + blocks - 1 + me // per, blocks))
+
+    send_block(lax.rem(blocks - 1 + me // per, blocks))
+    for part in range(PARTS):
+        keep(sig_out.at[part], sig_in.at[part], 1 + part).start()
+    for part in range(1, PARTS):
+        to_all(sig_out.at[part], sig_in.at[part], 2 + part)
+
+    all_copies(spec_out, spec_in, recv_sems.at[1]).wait()
     own_spec.wait()
     sf[...] = spec_in[...].astype(jnp.float32)
-    await_all(sig_out, sig_in, 2)
-    own_sig.wait()
-    xs[...] = sig_in[...].astype(jnp.float32)
-    transform(xs, sf, ys, tabs)
-    conv_out[...] = ys[...].astype(jnp.bfloat16)
-
-    own_conv = pltpu.make_async_copy(conv_out.at[me], conv_in.at[me], own_sems.at[2])
-    own_conv.start()
-
-    @pl.loop(1, group)
-    def _(k):
-        peer = lax.rem(me + k, group)
-        copy_to(conv_out.at[peer], conv_in.at[me], 3, peer).start()
-
-    await_all(conv_out, conv_in, 3)
-    own_conv.wait()
+    for part in range(PARTS):
+        all_copies(sig_out.at[part], sig_in.at[part], recv_sems.at[2 + part]).wait()
+        keep(sig_out.at[part], sig_in.at[part], 1 + part).wait()
+        xs[...] = sig_in[part].astype(jnp.float32)
+        transform(xs, sf, ys, tabs)
+        conv_out[part] = ys[...].astype(jnp.bfloat16)
+        keep(conv_out.at[part], conv_in.at[part], 1 + PARTS + part).start()
+        to_all(conv_out.at[part], conv_in.at[part], 2 + PARTS + part)
+
+    all_copies(spec_out, spec_in, send_sems.at[1]).wait()
+    for part in range(PARTS):
+        all_copies(sig_out.at[part], sig_in.at[part], send_sems.at[2 + part]).wait()
+    for part in range(PARTS):
+        number = 2 + PARTS + part
+        all_copies(conv_out.at[part], conv_in.at[part], send_sems.at[number]).wait()
+        all_copies(conv_out.at[part], conv_in.at[part], recv_sems.at[number]).wait()
+        keep(conv_out.at[part], conv_in.at[part], 1 + PARTS + part).wait()
 
     @pl.loop(0, blocks)
     def _(block):
         lanes = pl.ds(pl.multiple_of(block * COLS, COLS), COLS)
-        conv = conv_in[pl.ds(block * per, per)].reshape(COLS, COLS).astype(jnp.float32)
+        pieces = [
+            conv_in[part, pl.ds(block * per, per)].astype(jnp.float32)[:, None]
+            for part in range(PARTS)
+        ]
+        conv = jnp.concatenate(pieces, axis=1).reshape(COLS, COLS)
         skip = bias[:, lanes] * gated[:, lanes].astype(jnp.float32)
-        out[:, lanes] = q_keep[:, lanes] * (jnp.transpose(conv) + skip)
+        total[:, lanes] = jnp.transpose(conv) + skip
 
 
 def local(projected, conv_weight, bias, spectrum):
@@ -206,32 +227,32 @@
     bf16, f32 = jnp.bfloat16, jnp.float32
     made = tables(group)
     vmem = pl.BlockSpec(memory_space=pltpu.VMEM)
-    return pl.pallas_call(
+    q_short, total = pl.pallas_call(
         functools.partial(kernel, group),
-        out_shape=jax.ShapeDtypeStruct((rows, channels), f32),
+        out_shape=[jax.ShapeDtypeStruct((rows, channels), f32)] * 2,
         in_specs=[vmem] * (4 + len(made)),
-        out_specs=vmem,
+        out_specs=[vmem] * 2,
         scratch_shapes=[
             pltpu.VMEM((8, channels), bf16),
             pltpu.VMEM((8, channels), bf16),
-            pltpu.VMEM((rows, channels), f32),
             pltpu.VMEM((rows, channels), bf16),
-            pltpu.VMEM((group, SHARE, COLS), f32),
-            pltpu.VMEM((group, SHARE, COLS), f32),
+            pltpu.VMEM((group, PIECE, COLS), f32),
+            pltpu.VMEM((group, PIECE, COLS), f32),
             pltpu.VMEM((group, 4, COLS), f32),
-            pltpu.VMEM((group, SHARE, COLS), bf16),
-            pltpu.VMEM((group, SHARE, COLS), bf16),
+            pltpu.VMEM((PARTS, group, PIECE, COLS), bf16),
+            pltpu.VMEM((PARTS, group, PIECE, COLS), bf16),
             pltpu.VMEM((group, 4, COLS), bf16),
             pltpu.VMEM((group, 4, COLS), bf16),
-            pltpu.VMEM((group, SHARE, COLS), bf16),
-            pltpu.VMEM((group, SHARE, COLS), bf16),
-            pltpu.SemaphoreType.DMA((4,)),
-            pltpu.SemaphoreType.DMA((4,)),
-            pltpu.SemaphoreType.DMA((3,)),
+            pltpu.VMEM((PARTS, group, PIECE, COLS), bf16),
+            pltpu.VMEM((PARTS, group, PIECE, COLS), bf16),
+            pltpu.SemaphoreType.DMA((2 + 2 * PARTS,)),
+            pltpu.SemaphoreType.DMA((2 + 2 * PARTS,)),
+            pltpu.SemaphoreType.DMA((1 + 2 * PARTS,)),
         ],
         compiler_params=pltpu.CompilerParams(collective_id=0, has_side_effects=True),
         name="hyena",
     )(projected, conv_weight, bias[None, :], spectrum, *made)
+    return q_short * total
 
 
 def solution(mesh):

time: 69.2 us -> 63.1 us (0.912)
  Pallas kernels: 66.7 us -> 60.3 us
  other arithmetic: 0 us -> 2.64 us
  local copies, waits for them, and re-layouts: 2.3 us -> 0 us
    pallas_call x1, Pallas kernels: 66.7 us -> 60.3 us  [local(): pl.pallas_call(functools.partial(kernel, group), out_shape=[jax.ShapeDtyp...]
    mul x0 -> x1, other arithmetic: none -> 2.64 us  [local(): return q_short * total]
    unnamed x1 -> x0, local copies, waits for them, and re-layouts: 2.3 us -> none
where the time goes in v2:
time: 63.1 us; the launch traced here: 63 us
  Pallas kernels  60.3 us (96%)
  other arithmetic  2.64 us (4%)
    pallas_call x1, Pallas kernels, local(): pl.pallas_call(functools.partial(kernel, group), out_shape=[jax.ShapeDtyp...  60.3 us
    mul x1, other arithmetic, local(): return q_short * total  2.64 us

profile of v2, /device:TPU:1, one launch (start us, length us, event | category | flops | bytes accessed | tf_op | source)
XLA Modules:
  0.0 63.0 jit_solution(11425645038242878614)
XLA Ops:
  0.0 60.3 %hyena.1 = (f32[128,2048]{1,0:T(8,128)}, f32[128,2048]{1,0:T(8,128)}) custom-call(bf16[3,128,2048]{2,1,0:T(8,128)(2,1)} %proj.1, f32[3,3,2048]{2,1,0:T(4,128)} %weight.1, f32[1,2048]{1,0:T(1,128)} %bitcast.1, f32[2,2,128,128]{3,2,1,0:T(8,128)} %spec.1, bf16[512,256]{1,0:T(8,128)(2,1)} %constant.20.clone.refs_0_, bf16[512,256]{1,0:T(8,128)(2,1)} %constant.21.clone.refs_1_, ...), custom_call_target="tpu_custom_call" | custom-call | tf_op jit(solution)/shard_map/hyena/pallas_call | solution.py:230
  60.3 2.6 %mul.3 = f32[128,2048]{1,0:T(8,128)} multiply(f32[128,2048]{1,0:T(8,128)} %get-tuple-element.7, f32[128,2048]{1,0:T(8,128)} %get-tuple-element.8) | non-fusion elementwise | flops 262144 | bytes 3145728 | tf_op jit(solution)/shard_map/mul | solution.py:255

commit v3 on v2

--- a/solution.py
+++ b/solution.py
@@ -10,7 +10,7 @@
 
 COLS = 128
 SHARE = 16
-PARTS = 2
+PARTS = 4
 PIECE = SHARE // PARTS
 HALF = PIECE // 2
 
@@ -78,9 +78,9 @@
 
 def kernel(group, proj, weight, bias, spec, *refs):
     tabs = refs[:10]
-    q_keep, total = refs[10:12]
-    (tail, halo, gated, xs, ys, sf, sig_out, sig_in, spec_out, spec_in, conv_out, conv_in,
-     send_sems, recv_sems, own_sems) = refs[12:]
+    out = refs[10]
+    (tail, halo, q_keep, gated, xs, ys, sf, sig_out, sig_in, spec_out, spec_in, conv_out, conv_in,
+     send_sems, recv_sems, own_sems) = refs[11:]
     me = lax.axis_index("context")
     rows = proj.shape[1]
     blocks = proj.shape[2] // COLS
@@ -128,6 +128,25 @@
         for j in range(2):
             sf[:, 2 * i + j, :] = jnp.transpose(spec[i, j])
     spec_out[...] = sf[...].astype(jnp.bfloat16)
+    row = lax.broadcasted_iota(jnp.int32, (rows, COLS), 0)
+
+    def short(x, j, lanes, e2, e1):
+        n = row[: x.shape[0]]
+        x1 = jnp.where(n == 0, e1, pltpu.roll(x, 1, 0))
+        x2 = jnp.where(n == 0, e2, jnp.where(n == 1, e1, pltpu.roll(x, 2, 0)))
+        w = weight[j, :, lanes]
+        return w[0:1] * x + w[1:2] * x1 + w[2:3] * x2
+
+    @pl.loop(0, blocks)
+    def _(block):
+        lanes = pl.ds(pl.multiple_of(block * COLS, COLS), COLS)
+        none = jnp.zeros((1, COLS), jnp.float32)
+        q, k, v = [
+            short(proj[j, :, lanes].astype(jnp.float32), j, lanes, none, none) for j in range(3)
+        ]
+        q_keep[:, lanes] = q
+        gated[:, lanes] = (k * v).astype(jnp.bfloat16)
+
     pl.semaphore_wait(barrier, group - 1)
 
     @pl.when(me < group - 1)
@@ -155,25 +174,24 @@
             def _():
                 copy_to(sig_out.at[0, peer], sig_in.at[0, me], 2, peer).start()
 
-    row = lax.broadcasted_iota(jnp.int32, (rows, COLS), 0)
-
     @pl.loop(0, blocks)
     def _(step):
         block = lax.rem(step + me // per, blocks)
         lanes = pl.ds(pl.multiple_of(block * COLS, COLS), COLS)
         edge = halo[:, lanes].astype(jnp.float32)
-        shorts = []
-        for j in range(3):
-            x = proj[j, :, lanes].astype(jnp.float32)
-            e2, e1 = edge[2 * j : 2 * j + 1, :], edge[2 * j + 1 : 2 * j + 2, :]
-            x1 = jnp.where(row == 0, e1, pltpu.roll(x, 1, 0))
-            x2 = jnp.where(row == 0, e2, jnp.where(row == 1, e1, pltpu.roll(x, 2, 0)))
-            w = weight[j, :, lanes]
-            shorts.append(w[0:1] * x + w[1:2] * x1 + w[2:3] * x2)
-        q_keep[:, lanes] = shorts[0]
-        g = (shorts[1] * shorts[2]).astype(jnp.bfloat16)
-        gated[:, lanes] = g
-        turned = jnp.transpose(g.astype(jnp.float32))
+        q, k, v = [
+            short(
+                proj[j, 0:16, lanes].astype(jnp.float32),
+                j,
+                lanes,
+                edge[2 * j : 2 * j + 1, :],
+                edge[2 * j + 1 : 2 * j + 2, :],
+            )
+            for j in range(3)
+        ]
+        q_keep[0:16, lanes] = q
+        gated[0:16, lanes] = (k * v).astype(jnp.bfloat16)
+        turned = jnp.transpose(gated[:, lanes].astype(jnp.float32))
         turned = turned.reshape(per, PARTS, PIECE, COLS)
         for part in range(PARTS):
             sig_out[part, pl.ds(block * per, per)] = turned[:, part].astype(jnp.bfloat16)
@@ -200,6 +218,11 @@
         keep(conv_out.at[part], conv_in.at[part], 1 + PARTS + part).start()
         to_all(conv_out.at[part], conv_in.at[part], 2 + PARTS + part)
 
+    @pl.loop(0, blocks)
+    def _(block):
+        lanes = pl.ds(pl.multiple_of(block * COLS, COLS), COLS)
+        out[:, lanes] = bias[:, lanes] * gated[:, lanes].astype(jnp.float32)
+
     all_copies(spec_out, spec_in, send_sems.at[1]).wait()
     for part in range(PARTS):
         all_copies(sig_out.at[part], sig_in.at[part], send_sems.at[2 + part]).wait()
@@ -217,8 +240,7 @@
             for part in range(PARTS)
         ]
         conv = jnp.concatenate(pieces, axis=1).reshape(COLS, COLS)
-        skip = bias[:, lanes] * gated[:, lanes].astype(jnp.float32)
-        total[:, lanes] = jnp.transpose(conv) + skip
+        out[:, lanes] = q_keep[:, lanes] * (jnp.transpose(conv) + out[:, lanes])
 
 
 def local(projected, conv_weight, bias, spectrum):
@@ -227,14 +249,15 @@
     bf16, f32 = jnp.bfloat16, jnp.float32
     made = tables(group)
     vmem = pl.BlockSpec(memory_space=pltpu.VMEM)
-    q_short, total = pl.pallas_call(
+    return pl.pallas_call(
         functools.partial(kernel, group),
-        out_shape=[jax.ShapeDtypeStruct((rows, channels), f32)] * 2,
+        out_shape=jax.ShapeDtypeStruct((rows, channels), f32),
         in_specs=[vmem] * (4 + len(made)),
-        out_specs=[vmem] * 2,
+        out_specs=vmem,
         scratch_shapes=[
             pltpu.VMEM((8, channels), bf16),
             pltpu.VMEM((8, channels), bf16),
+            pltpu.VMEM((rows, channels), f32),
             pltpu.VMEM((rows, channels), bf16),
             pltpu.VMEM((group, PIECE, COLS), f32),
             pltpu.VMEM((group, PIECE, COLS), f32),
@@ -252,7 +275,6 @@
         compiler_params=pltpu.CompilerParams(collective_id=0, has_side_effects=True),
         name="hyena",
     )(projected, conv_weight, bias[None, :], spectrum, *made)
-    return q_short * total
 
 
 def solution(mesh):

time: 63.1 us -> 61.2 us (0.970)
  other arithmetic: 2.64 us -> 0 us
  local copies, waits for them, and re-layouts: 0 us -> 2.3 us
  Pallas kernels: 60.3 us -> 58.7 us
    mul x1 -> x0, other arithmetic: 2.64 us -> none  [local(): return q_short * total]
    unnamed x0 -> x1, local copies, waits for them, and re-layouts: none -> 2.3 us
    pallas_call x1, Pallas kernels: 60.3 us -> 58.7 us  [local(): pl.pallas_call(functools.partial(kernel, group), out_shape=jax.ShapeDtype...]
where the time goes in v3:
time: 61.2 us; the launch traced here: 61 us
  Pallas kernels  58.7 us (96%)
  local copies, waits for them, and re-layouts  2.3 us (4%)
    pallas_call x1, Pallas kernels, local(): pl.pallas_call(functools.partial(kernel, group), out_shape=jax.ShapeDtype...  58.7 us
    unnamed x1, local copies, waits for them, and re-layouts  2.3 us

profile of v3, /device:TPU:1, one launch (start us, length us, event | category | flops | bytes accessed | tf_op | source)
XLA Modules:
  0.0 61.0 jit_solution(12522296290664962320)
XLA Ops:
  0.0 58.7 %hyena.1 = f32[128,2048]{1,0:T(8,128)} custom-call(bf16[3,128,2048]{2,1,0:T(8,128)(2,1)} %proj.1, f32[3,3,2048]{2,1,0:T(4,128)} %weight.1, f32[1,2048]{1,0:T(1,128)} %bitcast.1, f32[2,2,128,128]{3,2,1,0:T(8,128)} %spec.1, bf16[512,256]{1,0:T(8,128)(2,1)} %constant.20.clone.refs_0_, bf16[512,256]{1,0:T(8,128)(2,1)} %constant.21.clone.refs_1_, ...), custom_call_target="tpu_custom_call" | custom-call | tf_op jit(solution)/shard_map/hyena/pallas_call | solution.py:252
  58.7 2.3 %copy.16 = f32[128,2048]{1,0:T(8,128)} copy(f32[128,2048]{1,0:T(8,128)} %hyena.1) | data formatting | bytes 2097152

commit v4 on v3

--- a/solution.py
+++ b/solution.py
@@ -76,11 +76,14 @@
             ys[:, h + i + HALF, :] = o[n:, i * COLS : (i + 1) * COLS]
 
 
-def kernel(group, proj, weight, bias, spec, *refs):
-    tabs = refs[:10]
-    out = refs[10]
-    (tail, halo, q_keep, gated, xs, ys, sf, sig_out, sig_in, spec_out, spec_in, conv_out, conv_in,
-     send_sems, recv_sems, own_sems) = refs[11:]
+def kernel(group, *refs):
+    given = refs[:14]
+    out = refs[14]
+    loaded = refs[15:29]
+    proj, weight, bias, spec = loaded[:4]
+    tabs = loaded[4:]
+    (load_sems, tail, halo, q_keep, gated, xs, ys, sf, sig_out, sig_in, spec_out, spec_in, conv_out, conv_in,
+     send_sems, recv_sems, own_sems) = refs[29:]
     me = lax.axis_index("context")
     rows = proj.shape[1]
     blocks = proj.shape[2] // COLS
@@ -121,6 +124,14 @@
             device_id_type=pl.DeviceIdType.MESH,
         )
 
+    loads = [
+        pltpu.make_async_copy(src, dst, load_sems.at[i])
+        for i, (src, dst) in enumerate(zip(given, loaded))
+    ]
+    for load in loads:
+        load.start()
+    for load in loads[:4]:
+        load.wait()
     ends = [proj[j, rows - 16 :, :].astype(jnp.float32)[14:16, :] for j in range(3)]
     ends.append(jnp.zeros_like(ends[0]))
     tail[...] = jnp.concatenate(ends, axis=0).astype(jnp.bfloat16)
@@ -147,6 +158,8 @@
         q_keep[:, lanes] = q
         gated[:, lanes] = (k * v).astype(jnp.bfloat16)
 
+    for load in loads[4:]:
+        load.wait()
     pl.semaphore_wait(barrier, group - 1)
 
     @pl.when(me < group - 1)
@@ -249,12 +262,15 @@
     bf16, f32 = jnp.bfloat16, jnp.float32
     made = tables(group)
     vmem = pl.BlockSpec(memory_space=pltpu.VMEM)
+    given = (projected, conv_weight, bias[None, :], spectrum, *made)
     return pl.pallas_call(
         functools.partial(kernel, group),
         out_shape=jax.ShapeDtypeStruct((rows, channels), f32),
-        in_specs=[vmem] * (4 + len(made)),
+        in_specs=[pl.BlockSpec(memory_space=pl.ANY)] * len(given),
         out_specs=vmem,
-        scratch_shapes=[
+        scratch_shapes=[pltpu.VMEM(x.shape, x.dtype) for x in given]
+        + [
+            pltpu.SemaphoreType.DMA((len(given),)),
             pltpu.VMEM((8, channels), bf16),
             pltpu.VMEM((8, channels), bf16),
             pltpu.VMEM((rows, channels), f32),
@@ -274,7 +290,7 @@
         ],
         compiler_params=pltpu.CompilerParams(collective_id=0, has_side_effects=True),
         name="hyena",
-    )(projected, conv_weight, bias[None, :], spectrum, *made)
+    )(*given)
 
 
 def solution(mesh):

time: 61.2 us -> 60.9 us (level)
  no operation moved by 1% of the time
where the time goes in v4:
time: 60.9 us; the launch traced here: 60.8 us
  Pallas kernels  58.5 us (96%)
  local copies, waits for them, and re-layouts  2.3 us (4%)
    pallas_call x1, Pallas kernels, local(): pl.pallas_call(functools.partial(kernel, group), out_shape=jax.ShapeDtype...  58.5 us
    unnamed x1, local copies, waits for them, and re-layouts  2.3 us

profile of v4, /device:TPU:1, one launch (start us, length us, event | category | flops | bytes accessed | tf_op | source)
XLA Modules:
  0.0 60.8 jit_solution(14984231199658776195)
XLA Ops:
  0.0 58.5 %hyena.1 = f32[128,2048]{1,0:T(8,128)} custom-call(bf16[3,128,2048]{2,1,0:T(8,128)(2,1)} %refs_0_.1, f32[3,3,2048]{2,1,0:T(4,128)} %refs_1_.1, f32[1,2048]{1,0:T(1,128)} %bitcast.1, f32[2,2,128,128]{3,2,1,0:T(8,128)} %refs_3_.1, bf16[512,256]{1,0:T(8,128)(2,1)} %constant.20.clone.refs_4_, bf16[512,256]{1,0:T(8,128)(2,1)} %constant.21.clone.refs_5_, ...), custom_call_target="tpu_custom_call" | custom-call | tf_op jit(solution)/shard_map/hyena/pallas_call | solution.py:266
  58.5 2.3 %copy.16 = f32[128,2048]{1,0:T(8,128)} copy(f32[128,2048]{1,0:T(8,128)} %hyena.1) | data formatting | bytes 2097152
